TPU v7x, 256 devices: a whole 4x4x8 slice. The times are simulated.
256 devices in a mesh: rep: 16 (over x, z_lo, core), tp: 16 (over z_hi, y).
Axes of the slice: x: 4, y: 4, z: 8 (z_hi: 4, z_lo: 2; z = z_hi * 2 + z_lo), core: 2. Of those that a mesh axis runs over, the one named last changes fastest.
Arguments:
- activations: bfloat16 [16, 256, 2560], P('rep', 'tp'), may hold values from -6 to 6
- out_grad: bfloat16 [16, 256, 2560], P('rep', 'tp'), may hold values from -6 to 6
- gate_weight: bfloat16 [16, 2560, 6912], P('rep', None, 'tp'), may hold values from -6 to 6
- up_weight: bfloat16 [16, 2560, 6912], P('rep', None, 'tp'), may hold values from -6 to 6
- down_weight: bfloat16 [16, 6912, 2560], P('rep', 'tp'), may hold values from -6 to 6
- step_index: int32 [1], replicated, may hold values from 0 to 999
Outputs:
- layer_out: bfloat16 [16, 256, 2560], P('rep', 'tp')
- grad_in: bfloat16 [16, 256, 2560], P('rep', 'tp')
- new_gate: bfloat16 [16, 2560, 6912], P('rep', None, 'tp')
- new_up: bfloat16 [16, 2560, 6912], P('rep', None, 'tp')
- new_down: bfloat16 [16, 6912, 2560], P('rep', 'tp')
All inputs are finite; a program needn't handle non-finite values.
Results may differ from a plain program's by a relative error of at most 0.0052.
Values may be sent and summed in bfloat16 or wider, within the bound.
A program may use at most 128 MiB of HBM per device.

v0:
```python
from functools import partial
import math
import jax
import jax.numpy as jnp
from jax import lax
from jax.sharding import PartitionSpec as P

D = 2560
FF = 6912
learn_rate = 0.8


def for_sending(x):

    def short(part):
        return part.astype(jnp.bfloat16) if part.dtype == jnp.float32 else part

    return jax.tree.map(short, x)


def shifted(x, axis, by):
    devices = lax.axis_size(axis)
    return lax.ppermute(x, axis, [(i, (i + by) % devices) for i in range(devices)])


def partner_copy(stepped, distance, loop_size):
    return shifted(
        (for_sending(stepped[0]), for_sending(stepped[1]), for_sending(stepped[2])), "rep", distance
    )


def shards(activations, out_grad, gate_weight, up_weight, down_weight, step_index):
    tokens_local = activations[0]
    grads_local = out_grad[0]
    gate_w = gate_weight[0]
    up_w = up_weight[0]
    down_w = down_weight[0]
    width_scale = 1.0 / math.sqrt(D)
    hidden_scale = 1.0 / math.sqrt(FF)
    gathered = lax.all_gather(tokens_local, "tp", axis=0, tiled=True)
    gate_pre = jnp.dot(gathered, gate_w, preferred_element_type=jnp.float32) * width_scale
    up_pre = jnp.dot(gathered, up_w, preferred_element_type=jnp.float32) * width_scale
    sigmoid_gate = jax.nn.sigmoid(gate_pre)
    activated = gate_pre * sigmoid_gate
    hidden = (activated * up_pre).astype(jnp.bfloat16)
    rows_hidden = hidden
    layer_part = lax.psum_scatter(
        jnp.dot(rows_hidden, down_w, preferred_element_type=jnp.float32) * hidden_scale,
        "tp",
        scatter_dimension=0,
        tiled=True,
    )
    piece = lax.all_gather(grads_local, "tp", axis=0, tiled=True)
    rows_hidden = hidden
    down_sum = jnp.einsum("tf,td->fd", rows_hidden, piece, preferred_element_type=jnp.float32)
    back_rows = jnp.einsum("td,fd->tf", piece, down_w, preferred_element_type=jnp.float32)
    down_sum, back_hidden = (down_sum, back_rows)
    grad_down = down_sum * hidden_scale
    d_hidden = back_hidden * hidden_scale
    d_gate = (d_hidden * up_pre * (sigmoid_gate * (1.0 + gate_pre * (1.0 - sigmoid_gate)))).astype(
        jnp.bfloat16
    )
    d_up = (d_hidden * activated).astype(jnp.bfloat16)
    grad_gate = (
        jnp.einsum("td,tf->df", gathered, d_gate, preferred_element_type=jnp.float32) * width_scale
    )
    grad_upw = (
        jnp.einsum("td,tf->df", gathered, d_up, preferred_element_type=jnp.float32) * width_scale
    )
    grad_part = lax.psum_scatter(
        (
            jnp.einsum("tf,df->td", d_gate, gate_w, preferred_element_type=jnp.float32)
            + jnp.einsum("tf,df->td", d_up, up_w, preferred_element_type=jnp.float32)
        )
        * width_scale,
        "tp",
        scatter_dimension=0,
        tiled=True,
    )
    stepped = (
        (gate_w.astype(jnp.float32) - learn_rate * grad_gate).astype(jnp.bfloat16),
        (up_w.astype(jnp.float32) - learn_rate * grad_upw).astype(jnp.bfloat16),
        (down_w.astype(jnp.float32) - learn_rate * grad_down).astype(jnp.bfloat16),
    )
    loop_size = lax.axis_size("rep")
    levels = loop_size.bit_length() - 1
    branches = [
        partial(partner_copy, distance=1 << level, loop_size=loop_size) for level in range(levels)
    ]
    chosen = step_index[0] % levels
    received = lax.switch(chosen, branches, stepped)
    averaged = tuple(
        (
            ((mine.astype(jnp.float32) + theirs.astype(jnp.float32)) * 0.5).astype(jnp.bfloat16)
            for mine, theirs in zip(stepped, received)
        )
    )
    return (
        layer_part.astype(jnp.bfloat16)[None],
        grad_part.astype(jnp.bfloat16)[None],
        averaged[0][None],
        averaged[1][None],
        averaged[2][None],
    )


def solution(mesh):
    in_specs = (
        P("rep", "tp", None),
        P("rep", "tp", None),
        P("rep", None, "tp"),
        P("rep", None, "tp"),
        P("rep", "tp", None),
        P(),
    )
    out_specs = (
        P("rep", "tp", None),
        P("rep", "tp", None),
        P("rep", None, "tp"),
        P("rep", None, "tp"),
        P("rep", "tp", None),
    )
    return jax.shard_map(shards, mesh=mesh, in_specs=in_specs, out_specs=out_specs, check_vma=False)
```

profile of v0, /device:TPU:6, one launch (start us, length us, event | category | flops | bytes accessed | tf_op | source)
XLA Modules:
  0.0 318.3 jit_solution(7605034518232308111)
XLA Ops:
  8.7 59.0 %all-gather.5.cloned.1.call-done = bf16[1,256,2560]{2,1,0:T(8,128)(2,1)} async-done(((bf16[1,16,2560]{2,1,0:T(8,128)(2,1)}), bf16[1,256,2560]{2,1,0:T(8,128)(2,1)}) %all-gather.5.cloned.1.call-update) | async-done | bytes 1310736 | tf_op jit(solution)/shard_map/all_gather | solution.py:40
  67.7 3.7 %fusion.39 = f32[256,432]{0,1:T(8,128)} fusion(bf16[1,2560,432]{1,2,0:T(8,128)(2,1)} %param.13, bf16[1,256,2560]{2,1,0:T(8,128)(2,1)} %all-gather.5.cloned.1.call-done), kind=kOutput, calls=%fused_computation.43 | convolution fusion | flops 566341632 | bytes 3964928 | tf_op jit(solution)/shard_map/dot_general | solution.py:42
  71.4 1.5 fusion.34
  72.9 48.9 %all-gather.7.cloned.1.call-done = bf16[1,256,2560]{2,1,0:T(8,128)(2,1)} async-done(((bf16[1,16,2560]{2,1,0:T(8,128)(2,1)}), bf16[1,256,2560]{2,1,0:T(8,128)(2,1)}) %all-gather.7.cloned.1.call-update) | async-done | bytes 1310736 | tf_op jit(solution)/shard_map/all_gather | solution.py:53
  121.8 3.2 %multiply_convert_fusion = (bf16[256,432]{0,1:T(8,128)(2,1)S(1)}, bf16[256,432]{0,1:T(8,128)(2,1)S(1)}, bf16[256,432]{0,1:T(8,128)(2,1)}) fusion(f32[256,432]{0,1:T(8,128)} %fusion.34, f32[256,432]{0,1:T(8,128)} %fusion.39, bf16[1,432,2560]{2,1,0:T(8,128)(2,1)S(1)} %copy-done, bf16[1,256,2560]{2,1,0:T(8,128)(2,1)} %all-gather.7.cloned.1.call-done), kind=kOutput, calls=%fused_computation.45 | convolution fusion | flops 568000512 | bytes 5070848 | tf_op jit(solution)/shard_map/td,fd->tf/dot_general | solution.py:56
  125.1 0.9 fusion.24
  125.9 0.9 copy-done.1
  126.8 2.4 fusion.14
  129.3 3.3 %convolution_multiply_fusion.3 = f32[256,2560]{1,0:T(8,128)} fusion(bf16[256,432]{0,1:T(8,128)(2,1)} %get-tuple-element.88, bf16[1,432,2560]{2,1,0:T(8,128)(2,1)S(1)} %copy-done), kind=kOutput, calls=%fused_computation.22 | convolution fusion | flops 566886400 | bytes 5054464 | tf_op jit(solution)/shard_map/dot_general | solution.py:48
  133.3 2.3 fusion.13
  136.5 1.6 copy-done.5
  138.1 2.1 fusion.12
  140.2 145.0 %conditional.4 = (bf16[2560,432]{0,1:T(8,128)(2,1)}, bf16[2560,432]{0,1:T(8,128)(2,1)}, bf16[432,2560]{1,0:T(8,128)(2,1)}) conditional(s32[]{:T(128)} %clamp.3, (bf16[2560,432]{0,1:T(8,128)(2,1)}, bf16[2560,432]{0,1:T(8,128)(2,1)S(1)}, bf16[432,2560]{1,0:T(8,128)(2,1)S(1)}) %tuple.58, (bf16[2560,432]{0,1:T(8,128)(2,1)}, ...), branch_computations={%region_2.3_spmd, %region_3.4_spmd, %region_4.5_spmd, %region_5.6_... | conditional | bytes 26542224
  140.2 1.5 collective-permute-start.9
  141.7 2.1 collective-permute-start.10
  143.8 1.5 collective-permute-start.11
  145.2 47.8 %collective-permute-done.9 = bf16[2560,432]{0,1:T(8,128)(2,1)} collective-permute-done((bf16[2560,432]{0,1:T(8,128)(2,1)}, bf16[2560,432]{0,1:T(8,128)(2,1)}, u32[]{:S(2)}, u32[]{:S(2)}) %collective-permute-start.9) | collective-permute-done | bytes 2211872 | tf_op jit(solution)/shard_map/cond/branch_3_fun/ppermute | solution.py:23
  193.0 47.4 %collective-permute-done.10 = bf16[2560,432]{0,1:T(8,128)(2,1)} collective-permute-done((bf16[2560,432]{0,1:T(8,128)(2,1)S(1)}, bf16[2560,432]{0,1:T(8,128)(2,1)}, u32[]{:S(2)}, u32[]{:S(2)}) %collective-permute-start.10) | collective-permute-done | bytes 2211872 | tf_op jit(solution)/shard_map/cond/branch_3_fun/ppermute | solution.py:23
  240.4 44.8 %collective-permute-done.11 = bf16[432,2560]{1,0:T(8,128)(2,1)} collective-permute-done((bf16[432,2560]{1,0:T(8,128)(2,1)S(1)}, bf16[432,2560]{1,0:T(8,128)(2,1)}, u32[]{:S(2)}, u32[]{:S(2)}) %collective-permute-start.11) | collective-permute-done | bytes 2211872 | tf_op jit(solution)/shard_map/cond/branch_3_fun/ppermute | solution.py:23
  285.3 4.3 %fusion.17 = bf16[1,432,2560]{2,1,0:T(8,128)(2,1)} fusion(bf16[432,2560]{1,0:T(8,128)(2,1)} %get-tuple-element.85, bf16[432,2560]{1,0:T(8,128)(2,1)} %copy-done.6), kind=kLoop, calls=%fused_computation.25 | loop fusion | flops 5529600 | bytes 6635520 | tf_op jit(solution)/shard_map/broadcast_in_dim | solution.py:103
  289.5 6.4 %fusion.15 = (bf16[1,2560,432]{1,2,0:T(8,128)(2,1)}, bf16[1,2560,432]{1,2,0:T(8,128)(2,1)}) fusion(bf16[2560,432]{0,1:T(8,128)(2,1)} %get-tuple-element.83, bf16[2560,432]{0,1:T(8,128)(2,1)} %fusion.12, bf16[2560,432]{0,1:T(8,128)(2,1)} %get-tuple-element.84, bf16[2560,432]{0,1:T(8,128)(2,1)S(1)} %fusion.11), kind=kLoop, calls=%fused_computation.23 | loop fusion | flops 11059200 | bytes 13271040 | tf_op jit(solution)/shard_map/broadcast_in_dim | solution.py:101
  295.9 1.6 convert_bitcast_fusion
  297.5 12.7 %reduce-scatter.3.cloned.1.call-done = f32[16,2560]{1,0:T(8,128)} async-done(((f32[256,2560]{1,0:T(8,128)}), f32[16,2560]{1,0:T(8,128)}) %reduce-scatter.3.cloned.1.call-update) | async-done | bytes 163856 | tf_op jit(solution)/shard_map/reduce_scatter | solution.py:47
  310.2 1.6 convert_bitcast_fusion.1
  (32 shorter events, 2.4 us)
Async XLA Ops:
  7.2 60.5 %all-gather.5.cloned.1.call-start = ((), (), s32[]{:S(2)}) async-start(), calls=%async_computation.4 | async-start | bytes 1392640 | tf_op jit(solution)/shard_map/all_gather | solution.py:40
  7.9 113.9 %all-gather.7.cloned.1.call-start = ((), (), s32[]{:S(2)}) async-start(), calls=%async_computation.5 | async-start | bytes 1392640 | tf_op jit(solution)/shard_map/all_gather | solution.py:53
  8.7 287.3 %reduce-scatter.5.cloned.1.call-start = ((), (), s32[]{:S(2)}) async-start(), calls=%async_computation.3 | async-start | bytes 2785280 | tf_op jit(solution)/shard_map/reduce_scatter | solution.py:70
  67.7 3.7 %copy-start.3 = (bf16[1,2560,432]{1,2,0:T(8,128)(2,1)S(1)}, bf16[1,2560,432]{1,2,0:T(8,128)(2,1)}, u32[]{:S(2)}) copy-start(bf16[1,2560,432]{1,2,0:T(8,128)(2,1)} %param.12) | copy-start | bytes 6635524
  67.7 3.7 %copy-start.7 = (bf16[1,256,2560]{2,1,0:T(8,128)(2,1)S(1)}, bf16[1,256,2560]{2,1,0:T(8,128)(2,1)}, u32[]{:S(2)}) copy-start(bf16[1,256,2560]{2,1,0:T(8,128)(2,1)} %all-gather.5.cloned.1.call-done) | copy-start | bytes 3932164
  71.4 50.5 %copy-start = (bf16[1,432,2560]{2,1,0:T(8,128)(2,1)S(1)}, bf16[1,432,2560]{2,1,0:T(8,128)(2,1)}, u32[]{:S(2)}) copy-start(bf16[1,432,2560]{2,1,0:T(8,128)(2,1)} %param.14) | copy-start | bytes 6635524
  121.8 3.2 %copy-start.4 = (bf16[1,2560,432]{1,2,0:T(8,128)(2,1)S(1)}, bf16[1,2560,432]{1,2,0:T(8,128)(2,1)}, u32[]{:S(2)}) copy-start(bf16[1,2560,432]{1,2,0:T(8,128)(2,1)} %param.12) | copy-start | bytes 6635524
  125.0 0.9 copy-start.8
  125.0 0.9 copy-start.10
  125.1 1.8 copy-start.1
  129.3 180.9 %reduce-scatter.3.cloned.1.call-start = ((), (), s32[]{:S(2)}) async-start(), calls=%async_computation.2 | async-start | bytes 2785280 | tf_op jit(solution)/shard_map/reduce_scatter | solution.py:47
  133.3 2.4 copy-start.2
  133.3 2.3 copy-start.11
  135.7 4.5 %copy-start.6 = (bf16[432,2560]{1,0:T(8,128)(2,1)}, bf16[432,2560]{1,0:T(8,128)(2,1)S(1)}, u32[]{:S(2)}) copy-start(bf16[432,2560]{1,0:T(8,128)(2,1)S(1)} %fusion.13) | copy-start | bytes 6635524
  135.7 2.4 copy-start.5
  135.7 2.4 copy-start.9
  140.2 52.8 %collective-permute-start.9 = (bf16[2560,432]{0,1:T(8,128)(2,1)}, bf16[2560,432]{0,1:T(8,128)(2,1)}, u32[]{:S(2)}, u32[]{:S(2)}) collective-permute-start(bf16[2560,432]{0,1:T(8,128)(2,1)} %get-tuple-element.51), channel_id=1, source_target_pairs={{0,128},{16,144},{32,160},{48,176},{64,192},{80,208},{96,224},{112... | collective-permute-start | bytes 6635528 | tf_op jit(solution)/shard_map/cond/branch_3_fun/ppermute | solution.py:23
  141.7 98.7 %collective-permute-start.10 = (bf16[2560,432]{0,1:T(8,128)(2,1)S(1)}, bf16[2560,432]{0,1:T(8,128)(2,1)}, u32[]{:S(2)}, u32[]{:S(2)}) collective-permute-start(bf16[2560,432]{0,1:T(8,128)(2,1)S(1)} %get-tuple-element.52), channel_id=1, source_target_pairs={{0,128},{16,144},{32,160},{48,176},{64,192},{80,208},{96,224},{112... | collective-permute-start | bytes 6635528 | tf_op jit(solution)/shard_map/cond/branch_3_fun/ppermute | solution.py:23
  143.8 141.5 %collective-permute-start.11 = (bf16[432,2560]{1,0:T(8,128)(2,1)S(1)}, bf16[432,2560]{1,0:T(8,128)(2,1)}, u32[]{:S(2)}, u32[]{:S(2)}) collective-permute-start(bf16[432,2560]{1,0:T(8,128)(2,1)S(1)} %get-tuple-element.53), channel_id=1, source_target_pairs={{0,128},{16,144},{32,160},{48,176},{64,192},{80,208},{96,224},{112... | collective-permute-start | bytes 6635528 | tf_op jit(solution)/shard_map/cond/branch_3_fun/ppermute | solution.py:23
Sparse Core Ops, SparseCore 0:
  10.4 57.2 all-gather.4
  70.1 51.7 all-gather.6
  129.4 88.2 reduce-scatter.4
  221.2 88.9 reduce-scatter.2
where the time goes:
time: 319 us; the launch traced here: 318 us
  waiting for transfers between devices  262 us (82%)
  matrix products  20.3 us (6%)
  between operations  14.5 us (5%)
  other arithmetic  13.8 us (4%)
  starting transfers between devices  5.14 us (2%)
    ppermute x3, waiting for transfers between devices, shifted(): lax.ppermute(x, axis, [(i, (i + by) % devices) for i in range(devices)])  140 us
    all_gather x1, waiting for transfers between devices, shards(): gathered = lax.all_gather(tokens_local, 'tp', axis=0, tiled=True)  59 us
    all_gather x1, waiting for transfers between devices, shards(): piece = lax.all_gather(grads_local, 'tp', axis=0, tiled=True)  48.9 us
    reduce_scatter x1, waiting for transfers between devices, shards(): lax.psum_scatter(jnp.dot(rows_hidden, down_w, preferred_element_type=jnp....  12.7 us
  transfers between devices with their start and end apart: 7, of which 6 were waited for; matrix products, arithmetic and copies ran while one was open for 8% of the time, Pallas kernels for 0%

commit v1 on v0

--- a/solution.py
+++ b/solution.py
@@ -37,7 +37,8 @@
     down_w = down_weight[0]
     width_scale = 1.0 / math.sqrt(D)
     hidden_scale = 1.0 / math.sqrt(FF)
-    gathered = lax.all_gather(tokens_local, "tp", axis=0, tiled=True)
+    repeated = jnp.stack([tokens_local] * lax.axis_size("tp"))
+    gathered = jnp.concatenate(lax.all_to_all(repeated, "tp", 0, 0), axis=0)
     gate_pre = jnp.dot(gathered, gate_w, preferred_element_type=jnp.float32) * width_scale
     up_pre = jnp.dot(gathered, up_w, preferred_element_type=jnp.float32) * width_scale
     sigmoid_gate = jax.nn.sigmoid(gate_pre)

time: 319 us -> 282 us (0.88)
  waiting for transfers between devices: 262 us -> 213 us
  starting transfers between devices: 5.14 us -> 16.3 us
    all_gather x1 -> x0, waiting for transfers between devices: 59 us -> none  [shards(): gathered = lax.all_gather(tokens_local, 'tp', axis=0, tiled=True)]
    all_to_all x0 -> x1, waiting for transfers between devices: none -> 33.6 us  [shards(): gathered = jnp.concatenate(lax.all_to_all(repeated, 'tp', 0, 0), axis=0)]
    all_gather x1, waiting for transfers between devices: 48.9 us -> 26.7 us  [shards(): piece = lax.all_gather(grads_local, 'tp', axis=0, tiled=True)]
    all_to_all x0 -> x1, starting transfers between devices: none -> 11.2 us  [shards(): gathered = jnp.concatenate(lax.all_to_all(repeated, 'tp', 0, 0), axis=0)]
where the time goes in v1:
time: 282 us
  waiting for transfers between devices  213 us (76%)
  matrix products  19.1 us (7%)
  starting transfers between devices  16.3 us (6%)
  between operations  14.5 us (5%)
  other arithmetic  13.2 us (5%)
  local copies, waits for them, and re-layouts  5.24 us (2%)
    ppermute x3, waiting for transfers between devices, shifted(): lax.ppermute(x, axis, [(i, (i + by) % devices) for i in range(devices)])  140 us
    all_to_all x1, waiting for transfers between devices, shards(): gathered = jnp.concatenate(lax.all_to_all(repeated, 'tp', 0, 0), axis=0)  33.6 us
    all_gather x1, waiting for transfers between devices, shards(): piece = lax.all_gather(grads_local, 'tp', axis=0, tiled=True)  26.7 us
    reduce_scatter x1, waiting for transfers between devices, shards(): lax.psum_scatter(jnp.dot(rows_hidden, down_w, preferred_element_type=jnp....  12.5 us
    all_to_all x1, starting transfers between devices, shards(): gathered = jnp.concatenate(lax.all_to_all(repeated, 'tp', 0, 0), axis=0)  11.2 us
    broadcast_in_dim x1, other arithmetic, shards(): averaged[0][None]  5.69 us
  transfers between devices with their start and end apart: 7, of which 6 were waited for; matrix products, arithmetic and copies ran while one was open for 8% of the time, Pallas kernels for 0%

profile of v1, /device:TPU:6, one launch (start us, length us, event | category | flops | bytes accessed | tf_op | source)
XLA Modules:
  0.0 281.7 jit_solution(500434462123670620)
XLA Ops:
  7.2 2.2 stack.3
  9.4 11.2 %all-to-all-start = ((bf16[16,16,2560]{2,1,0:T(8,128)(2,1)}), bf16[16,16,2560]{2,1,0:T(8,128)(2,1)S(1)}, u32[]{:S(2)}, u32[]{:S(2)}) async-start(bf16[16,16,2560]{2,1,0:T(8,128)(2,1)} %stack.3), calls=%async_computation | async-start | bytes 2621440 | tf_op jit(solution)/shard_map/all_to_all | solution.py:41
  21.4 33.6 %all-to-all-done = bf16[16,16,2560]{2,1,0:T(8,128)(2,1)S(1)} async-done(((bf16[16,16,2560]{2,1,0:T(8,128)(2,1)}), bf16[16,16,2560]{2,1,0:T(8,128)(2,1)S(1)}, u32[]{:S(2)}, u32[]{:S(2)}) %all-to-all-start) | async-done | bytes 1310752 | tf_op jit(solution)/shard_map/all_to_all | solution.py:41
  55.0 1.5 fusion.33
  56.6 1.5 fusion.30
  58.2 26.7 %all-gather.3.cloned.1.call-done = bf16[1,256,2560]{2,1,0:T(8,128)(2,1)} async-done(((bf16[1,16,2560]{2,1,0:T(8,128)(2,1)}), bf16[1,256,2560]{2,1,0:T(8,128)(2,1)}) %all-gather.3.cloned.1.call-update) | async-done | bytes 1310736 | tf_op jit(solution)/shard_map/all_gather | solution.py:54
  84.9 3.9 %multiply_convert_fusion = (bf16[256,432]{0,1:T(8,128)(2,1)S(1)}, bf16[256,432]{0,1:T(8,128)(2,1)S(1)}, bf16[256,432]{0,1:T(8,128)(2,1)}) fusion(f32[256,432]{0,1:T(8,128)} %fusion.30, f32[256,432]{0,1:T(8,128)} %fusion.33, bf16[1,432,2560]{2,1,0:T(8,128)(2,1)} %param.14, bf16[1,256,2560]{2,1,0:T(8,128)(2,1)} %all-gather.3.cloned.1.call-done), kind=kOutput, calls=%fused_computation.41 | convolution fusion | flops 568000512 | bytes 5070848 | tf_op jit(solution)/shard_map/td,fd->tf/dot_general | solution.py:57
  89.6 2.4 fusion.14
  92.2 1.5 copy-done.6
  93.7 3.3 %convolution_multiply_fusion.3 = f32[256,2560]{1,0:T(8,128)} fusion(bf16[256,432]{0,1:T(8,128)(2,1)} %get-tuple-element.88, bf16[1,432,2560]{2,1,0:T(8,128)(2,1)S(1)} %copy-done.6), kind=kOutput, calls=%fused_computation.22 | convolution fusion | flops 566886400 | bytes 5054464 | tf_op jit(solution)/shard_map/dot_general | solution.py:49
  97.7 2.6 fusion.11
  102.5 2.1 fusion.13
  104.7 144.7 %conditional.4 = (bf16[2560,432]{0,1:T(8,128)(2,1)}, bf16[2560,432]{0,1:T(8,128)(2,1)}, bf16[432,2560]{1,0:T(8,128)(2,1)}) conditional(s32[]{:T(128)} %clamp.3, (bf16[2560,432]{0,1:T(8,128)(2,1)S(1)}, bf16[2560,432]{0,1:T(8,128)(2,1)S(1)}, bf16[432,2560]{1,0:T(8,128)(2,1)}) %tuple.58, ...), branch_computations={%region_2.3_spmd, %region_3.4_spmd, %region_4.5_spmd, %region_5.6_... | conditional | bytes 26542224
  104.7 1.4 collective-permute-start.9
  106.1 2.1 collective-permute-start.10
  108.2 1.4 collective-permute-start.11
  109.6 47.6 %collective-permute-done.9 = bf16[2560,432]{0,1:T(8,128)(2,1)} collective-permute-done((bf16[2560,432]{0,1:T(8,128)(2,1)S(1)}, bf16[2560,432]{0,1:T(8,128)(2,1)}, u32[]{:S(2)}, u32[]{:S(2)}) %collective-permute-start.9) | collective-permute-done | bytes 2211872 | tf_op jit(solution)/shard_map/cond/branch_3_fun/ppermute | solution.py:23
  157.2 47.4 %collective-permute-done.10 = bf16[2560,432]{0,1:T(8,128)(2,1)} collective-permute-done((bf16[2560,432]{0,1:T(8,128)(2,1)S(1)}, bf16[2560,432]{0,1:T(8,128)(2,1)}, u32[]{:S(2)}, u32[]{:S(2)}) %collective-permute-start.10) | collective-permute-done | bytes 2211872 | tf_op jit(solution)/shard_map/cond/branch_3_fun/ppermute | solution.py:23
  204.6 44.7 %collective-permute-done.11 = bf16[432,2560]{1,0:T(8,128)(2,1)} collective-permute-done((bf16[432,2560]{1,0:T(8,128)(2,1)}, bf16[432,2560]{1,0:T(8,128)(2,1)}, u32[]{:S(2)}, u32[]{:S(2)}) %collective-permute-start.11) | collective-permute-done | bytes 2211872 | tf_op jit(solution)/shard_map/cond/branch_3_fun/ppermute | solution.py:23
  249.3 4.4 %fusion.17 = bf16[1,432,2560]{2,1,0:T(8,128)(2,1)} fusion(bf16[432,2560]{1,0:T(8,128)(2,1)} %get-tuple-element.85, bf16[432,2560]{1,0:T(8,128)(2,1)} %fusion.13), kind=kLoop, calls=%fused_computation.25 | loop fusion | flops 5529600 | bytes 6635520 | tf_op jit(solution)/shard_map/broadcast_in_dim | solution.py:104
  253.8 5.7 %fusion.15 = (bf16[1,2560,432]{1,2,0:T(8,128)(2,1)}, bf16[1,2560,432]{1,2,0:T(8,128)(2,1)}) fusion(bf16[2560,432]{0,1:T(8,128)(2,1)} %get-tuple-element.83, bf16[2560,432]{0,1:T(8,128)(2,1)S(1)} %copy-done.1, bf16[2560,432]{0,1:T(8,128)(2,1)} %get-tuple-element.84, bf16[2560,432]{0,1:T(8,128)(2,1)S(1)} %fusion.11), kind=kLoop, calls=%fused_computation.23 | loop fusion | flops 11059200 | bytes 13271040 | tf_op jit(solution)/shard_map/broadcast_in_dim | solution.py:102
  259.5 1.6 convert_bitcast_fusion
  261.0 12.5 %reduce-scatter.3.cloned.1.call-done = f32[16,2560]{1,0:T(8,128)} async-done(((f32[256,2560]{1,0:T(8,128)}), f32[16,2560]{1,0:T(8,128)}) %reduce-scatter.3.cloned.1.call-update) | async-done | bytes 163856 | tf_op jit(solution)/shard_map/reduce_scatter | solution.py:48
  273.6 1.6 convert_bitcast_fusion.1
  (34 shorter events, 4.0 us)
Async XLA Ops:
  7.2 47.9 %copy-start.2 = (bf16[1,2560,432]{1,2,0:T(8,128)(2,1)S(1)}, bf16[1,2560,432]{1,2,0:T(8,128)(2,1)}, u32[]{:S(2)}) copy-start(bf16[1,2560,432]{1,2,0:T(8,128)(2,1)} %param.13) | copy-start | bytes 6635524
  9.4 45.6 %all-to-all-start = ((bf16[16,16,2560]{2,1,0:T(8,128)(2,1)}), bf16[16,16,2560]{2,1,0:T(8,128)(2,1)S(1)}, u32[]{:S(2)}, u32[]{:S(2)}) async-start(bf16[16,16,2560]{2,1,0:T(8,128)(2,1)} %stack.3), calls=%async_computation | async-start | bytes 2621440 | tf_op jit(solution)/shard_map/all_to_all | solution.py:41
  20.6 64.3 %all-gather.3.cloned.1.call-start = ((), (), s32[]{:S(2)}) async-start(), calls=%async_computation.5 | async-start | bytes 1392640 | tf_op jit(solution)/shard_map/all_gather | solution.py:54
  21.3 238.1 %reduce-scatter.5.cloned.1.call-start = ((), (), s32[]{:S(2)}) async-start(), calls=%async_computation.4 | async-start | bytes 2785280 | tf_op jit(solution)/shard_map/reduce_scatter | solution.py:71
  55.0 1.6 copy-start.3
  84.9 3.9 %copy-start.4 = (bf16[1,2560,432]{1,2,0:T(8,128)(2,1)S(1)}, bf16[1,2560,432]{1,2,0:T(8,128)(2,1)}, u32[]{:S(2)}) copy-start(bf16[1,2560,432]{1,2,0:T(8,128)(2,1)} %param.12) | copy-start | bytes 6635524
  88.7 0.9 copy-start.9
  88.7 0.9 copy-start.11
  92.1 1.6 copy-start.6
  92.1 181.5 %reduce-scatter.3.cloned.1.call-start = ((), (), s32[]{:S(2)}) async-start(), calls=%async_computation.3 | async-start | bytes 2785280 | tf_op jit(solution)/shard_map/reduce_scatter | solution.py:48
  97.7 2.7 copy-start.5
  97.7 2.7 copy-start.10
  100.4 1.7 copy-start.7
  100.4 1.7 copy-start.8
  100.4 2.1 copy-start.12
  102.5 2.1 copy-start
  104.7 52.6 %collective-permute-start.9 = (bf16[2560,432]{0,1:T(8,128)(2,1)S(1)}, bf16[2560,432]{0,1:T(8,128)(2,1)}, u32[]{:S(2)}, u32[]{:S(2)}) collective-permute-start(bf16[2560,432]{0,1:T(8,128)(2,1)S(1)} %get-tuple-element.51), channel_id=1, source_target_pairs={{0,128},{16,144},{32,160},{48,176},{64,192},{80,208},{96,224},{112... | collective-permute-start | bytes 6635528 | tf_op jit(solution)/shard_map/cond/branch_3_fun/ppermute | solution.py:23
  106.1 98.5 %collective-permute-start.10 = (bf16[2560,432]{0,1:T(8,128)(2,1)S(1)}, bf16[2560,432]{0,1:T(8,128)(2,1)}, u32[]{:S(2)}, u32[]{:S(2)}) collective-permute-start(bf16[2560,432]{0,1:T(8,128)(2,1)S(1)} %get-tuple-element.52), channel_id=1, source_target_pairs={{0,128},{16,144},{32,160},{48,176},{64,192},{80,208},{96,224},{112... | collective-permute-start | bytes 6635528 | tf_op jit(solution)/shard_map/cond/branch_3_fun/ppermute | solution.py:23
  108.2 141.2 %collective-permute-start.11 = (bf16[432,2560]{1,0:T(8,128)(2,1)}, bf16[432,2560]{1,0:T(8,128)(2,1)}, u32[]{:S(2)}, u32[]{:S(2)}) collective-permute-start(bf16[432,2560]{1,0:T(8,128)(2,1)} %get-tuple-element.53), channel_id=1, source_target_pairs={{0,128},{16,144},{32,160},{48,176},{64,192},{80,208},{96,224},{112... | collective-permute-start | bytes 6635528 | tf_op jit(solution)/shard_map/cond/branch_3_fun/ppermute | solution.py:23
  249.3 4.4 %copy-start.1 = (bf16[2560,432]{0,1:T(8,128)(2,1)S(1)}, bf16[2560,432]{0,1:T(8,128)(2,1)}, u32[]{:S(2)}) copy-start(bf16[2560,432]{0,1:T(8,128)(2,1)} %copy-done) | copy-start | bytes 6635524
Sparse Core Ops, SparseCore 0:
  23.8 60.9 all-gather.2
  92.2 88.7 reduce-scatter.4
  184.6 88.9 reduce-scatter.2
